TPU v7x, 32 devices: a whole 2x2x4 slice. The times are simulated.
32 devices in a mesh: grp: 2 (over y), ctx: 4 (over z), head: 4 (over x, core).
Axes of the slice: x: 2, y: 2, z: 4, core: 2. Of those that a mesh axis runs over, the one named last changes fastest.
Arguments:
- inputs: bfloat16 [8192, 2560], P(('grp', 'ctx'), 'head'), parts along dimension 0, may hold values from -0.29882812 to 0.29882812
- write_coeffs: bfloat16 [8192, 128], P(('grp', 'ctx')), parts along dimension 0, may hold values from -1.796875 to 1.796875
- read_coeffs: bfloat16 [8192, 128], P(('grp', 'ctx')), parts along dimension 0, may hold values from -1.796875 to 1.796875
- log_decay: float32 [8192, 40], P(('grp', 'ctx'), 'head'), parts along dimension 0, may hold values from -1.6 to 0
- out_grad: bfloat16 [8192, 2560], P(('grp', 'ctx'), 'head'), parts along dimension 0, may hold values from -0.29882812 to 0.29882812
Outputs:
- outputs: bfloat16 [8192, 2560], P(('grp', 'ctx'), 'head'), parts along dimension 0
- in_grad: bfloat16 [8192, 2560], P(('grp', 'ctx'), 'head'), parts along dimension 0
- write_grad: float32 [8192, 128], P(('grp', 'ctx')), parts along dimension 0
- read_grad: float32 [8192, 128], P(('grp', 'ctx')), parts along dimension 0
- decay_grad: float32 [8192, 40], P(('grp', 'ctx'), 'head'), parts along dimension 0
There are 2 independent parts, one for each index of `grp`. A program takes and returns all parts, laid end to end along the dimension named above; each array names one. Nothing has to cross between parts.
All inputs are finite; a program needn't handle non-finite values.
Results may differ from a plain program's by a relative error of at most 0.0071.
Values sent between devices are 32-bit elements; how exact they have to be, the bound alone decides.
A program may use at most 64 MiB of HBM per device.

v0:
```python
import jax
import jax.numpy as jnp
from jax import lax
from jax.sharding import PartitionSpec as P

HEAD_DIM = 64
STATE = 128
BLOCK = 256


def entering_2(part, axis, combine, identity, reverse):
    count = lax.axis_size(axis)
    place = lax.axis_index(axis)
    ahead = count - 1 - place if reverse else place
    gathered = jax.tree.map(lambda a: lax.all_gather(a, axis), part)
    state = jax.tree.map(lambda a, e: jnp.zeros_like(a) + jnp.asarray(e, a.dtype), part, identity)

    def one(hop, state):
        source = count - 1 - hop if reverse else hop
        return combine(
            state, jax.tree.map(lambda a: lax.dynamic_index_in_dim(a, source, 0, False), gathered)
        )

    return lax.fori_loop(0, ahead, one, state)


def rounded(values):
    return values.astype(jnp.bfloat16)


def chain_step(former, latter):
    return (former[0] * latter[0], latter[0][:, None, None] * former[1] + latter[1])


def added(former, latter):
    return former + latter


def exact_product(form, left, right):
    return jnp.einsum(form, left, right, precision=lax.Precision.HIGHEST)


def per_device(inputs, write_coeffs, read_coeffs, log_decay, out_grad):
    tokens = inputs.shape[0]
    heads = log_decay.shape[1]
    blocks = tokens // BLOCK
    x_blocks = inputs.reshape(blocks, BLOCK, heads, HEAD_DIM)
    dy_blocks = out_grad.reshape(blocks, BLOCK, heads, HEAD_DIM)
    b_blocks = write_coeffs.reshape(blocks, BLOCK, STATE)
    c_blocks = read_coeffs.reshape(blocks, BLOCK, STATE)
    running = jnp.cumsum(log_decay.reshape(blocks, BLOCK, heads), axis=1)
    totals = running[:, -1:, :]
    across = jnp.swapaxes(running, 1, 2)
    spread = across[:, :, :, None] - across[:, :, None, :]
    causal = jnp.arange(BLOCK)[:, None] >= jnp.arange(BLOCK)[None, :]
    decays = jnp.where(causal, jnp.exp(jnp.where(causal, spread, 0.0)), 0.0)
    scores = jnp.einsum("ctn,csn->cts", c_blocks, b_blocks, preferred_element_type=jnp.float32)
    weights = rounded(scores[:, None] * decays)
    y_inner = jnp.einsum("chts,cshp->cthp", weights, x_blocks, preferred_element_type=jnp.float32)
    dx_inner = jnp.einsum("chts,cthp->cshp", weights, dy_blocks, preferred_element_type=jnp.float32)
    pairs = jnp.einsum("cthp,cshp->chts", dy_blocks, x_blocks, preferred_element_type=jnp.float32)
    pair_weights = rounded(pairs * decays)
    dc_inner = jnp.einsum(
        "chts,csn->ctn", pair_weights, b_blocks, preferred_element_type=jnp.float32
    )
    db_inner = jnp.einsum(
        "chts,ctn->csn", pair_weights, c_blocks, preferred_element_type=jnp.float32
    )
    grow = jnp.exp(running)[..., None]
    shrink = jnp.exp(totals - running)[..., None]
    x_wide = x_blocks.astype(jnp.float32)
    dy_wide = dy_blocks.astype(jnp.float32)
    block_states = jnp.einsum(
        "csn,cshp->chnp", b_blocks, rounded(x_wide * shrink), preferred_element_type=jnp.float32
    )
    block_adjoints = jnp.einsum(
        "ctn,cthp->chnp", c_blocks, rounded(dy_wide * grow), preferred_element_type=jnp.float32
    )
    gains = jnp.exp(totals[:, 0, :])
    empty = jnp.zeros((heads, STATE, HEAD_DIM), jnp.float32)
    dev_state = empty
    for index in range(blocks):
        dev_state = gains[index][:, None, None] * dev_state + block_states[index]
    dev_adjoint = empty
    for index in reversed(range(blocks)):
        dev_adjoint = gains[index][:, None, None] * dev_adjoint + block_adjoints[index]
    dev_gain = jnp.prod(gains, axis=0)
    identity = (jnp.ones_like(dev_gain), empty)
    incoming = entering_2((dev_gain, dev_state), "ctx", chain_step, identity, False)[1]
    outgoing = entering_2((dev_gain, dev_adjoint), "ctx", chain_step, identity, True)[1]
    carried = incoming
    entering = []
    for index in range(blocks):
        entering.append(carried)
        carried = gains[index][:, None, None] * carried + block_states[index]
    carried = outgoing
    leaving = [empty] * blocks
    for index in reversed(range(blocks)):
        leaving[index] = carried
        carried = gains[index][:, None, None] * carried + block_adjoints[index]
    states_in = jnp.stack(entering)
    adjoints_out = jnp.stack(leaving)
    y_full = y_inner + grow * exact_product(
        "ctn,chnp->cthp", c_blocks.astype(jnp.float32), states_in
    )
    dx_full = dx_inner + shrink * exact_product(
        "csn,chnp->cshp", b_blocks.astype(jnp.float32), adjoints_out
    )
    dc_full = dc_inner + exact_product("cthp,chnp->ctn", dy_wide * grow, states_in)
    db_full = db_inner + exact_product("cshp,chnp->csn", x_wide * shrink, adjoints_out)
    write_grad, read_grad = lax.psum(
        (db_full.reshape(tokens, STATE), dc_full.reshape(tokens, STATE)), "head"
    )
    balance = jnp.sum(dy_wide * y_full, axis=-1) - jnp.sum(x_wide * dx_full, axis=-1)
    balance = balance.reshape(tokens, heads)
    suffix = jnp.flip(jnp.cumsum(jnp.flip(balance, 0), axis=0), 0)
    later_sum = entering_2(
        jnp.sum(balance, axis=0), "ctx", added, jnp.zeros((heads,), jnp.float32), True
    )
    decay_grad = suffix + later_sum[None, :]
    outputs = rounded(y_full).reshape(tokens, heads * HEAD_DIM)
    in_grad = rounded(dx_full).reshape(tokens, heads * HEAD_DIM)
    return (outputs, in_grad, write_grad, read_grad, decay_grad)


def solution(mesh):
    in_specs = (
        P(("grp", "ctx"), "head"),
        P(("grp", "ctx"), None),
        P(("grp", "ctx"), None),
        P(("grp", "ctx"), "head"),
        P(("grp", "ctx"), "head"),
    )
    out_specs = (
        P(("grp", "ctx"), "head"),
        P(("grp", "ctx"), "head"),
        P(("grp", "ctx"), None),
        P(("grp", "ctx"), None),
        P(("grp", "ctx"), "head"),
    )
    return jax.shard_map(
        per_device, mesh=mesh, in_specs=in_specs, out_specs=out_specs, check_vma=False
    )
```

profile of v0, /device:TPU:0, one launch (start us, length us, event | category | flops | bytes accessed | tf_op | source)
XLA Modules:
  0.0 173.6 jit_solution(2918712966802886231)
XLA Ops:
  7.2 1.0 reshape.96
  8.3 2.3 %reduce-window.14 = f32[4,10,2,128]{3,1,2,0:T(8,128)S(1)} reduce-window(f32[4,10,2,128]{3,1,2,0:T(8,128)S(1)} %copy.87, f32[]{:T(128)} %constant.85.clone.1), window={size=1x1x1x128 pad=0_0x0_0x0_0x127_0}, to_apply=%region_0.0 | reduce-window | flops 1300480 | bytes 81924 | tf_op jit(solution)/shard_map/reduce-window
  11.5 0.7 copy.93
  12.1 1.9 %reshape.99 = bf16[4,256,10,64]{1,0,3,2:T(4,128)(2,1)} reshape(bf16[1024,640]{0,1:T(8,128)(2,1)S(1)} %copy.93) | data formatting | bytes 2621440 | tf_op jit(solution)/shard_map/reshape | solution.py:47
  14.0 0.6 copy.104
  14.7 1.9 %reshape.101 = bf16[4,256,10,64]{1,0,3,2:T(4,128)(2,1)} reshape(bf16[1024,640]{0,1:T(8,128)(2,1)S(1)} %copy.104) | data formatting | bytes 2621440 | tf_op jit(solution)/shard_map/reshape | solution.py:48
  16.6 0.5 convolution_bitcast_fusion.1
  17.1 0.8 copy-done.9
  17.9 0.5 convolution_bitcast_fusion
  18.4 1.2 slice_add_fusion
  19.7 0.7 all-gather.5.cloned.1.call-update
  20.6 0.6 dynamic-slice
  21.8 0.2 dynamic-update-slice
  22.1 13.6 %all-reduce = f32[40]{0:T(128)S(1)} all-reduce(f32[40]{0:T(128)S(1)} %dynamic-update-slice), channel_id=2, replica_groups=mesh['grp'=2,'ctx'=4,'head'=4] {'ctx'}, use_global_device_ids=true, to_apply=%add | all-reduce | flops 40 | bytes 320
  35.7 1.3 fusion.42
  37.0 0.2 copy-done.10
  37.2 5.0 %convert_reduce_fusion = bf16[4,256,256]{2,1,0:T(8,128)(2,1)} fusion(f32[4,10,256]{2,1,0:T(8,128)S(1)} %copy.91, pred[256,256]{1,0:T(8,128)(4,1)S(1)} %iota_compare_fusion, bf16[4,256,10,64]{1,0,3,2:T(4,128)(2,1)S(1)} %copy-done.10, bf16[4,256,10,64]{1,0,3,2:T(4,128)(2,1)S(1)} %copy-done.7), kind=kOutput, calls=%fused_computation.7 | convolution fusion | flops 353632256 | bytes 3252224 | tf_op jit(solution)/shard_map/cthp,cshp->chts/dot_general | solution.py:61
  42.2 13.1 %all-gather.7.cloned.1.call-done = f32[4,10,128,64]{2,3,1,0:T(8,128)} async-done(((f32[1,10,128,64]{2,3,1,0:T(8,128)}), f32[4,10,128,64]{2,3,1,0:T(8,128)}) %all-gather.7.cloned.1.call-update) | async-done | bytes 1310736 | tf_op jit(solution)/shard_map/all_gather | solution.py:15
  55.3 4.4 %while.39 = (s32[]{:T(128)}, f32[10,128,64]{2,1,0:T(8,128)S(1)}, s32[]{:T(128)}, f32[4,10]{1,0:T(4,128)S(1)}, f32[4,10,128,64]{2,3,1,0:T(8,128)}, /*index=5*/s32[]{:T(128)}, s32[]{:T(128)}, s32[]{:T(128)}, s32[]{:T(128)}) while((s32[]{:T(128)}, f32[10,128,64]{2,1,0:T(8,128)S(1)}, s32[]{:T(128)}, f32[4,10]{1,0:T(4,128)S(1)}, ...), condition=%wide.region_6.7_spmd, body=%wide.region_5.6_spmd.sunk | while | flops 163846 | bytes 2294035 | solution.py:24
  55.4 1.0 constant_dynamic-slice_fusion.5
  56.8 1.0 constant_dynamic-slice_fusion.5
  57.8 0.2 copy.166
  58.3 1.0 constant_dynamic-slice_fusion.5
  59.9 28.7 %all-gather.5.cloned.1.call-done = f32[4,10,128,64]{2,3,1,0:T(8,128)} async-done(((f32[1,10,128,64]{2,3,1,0:T(8,128)}), f32[4,10,128,64]{2,3,1,0:T(8,128)}) %all-gather.5.cloned.1.call-update) | async-done | bytes 1310736 | tf_op jit(solution)/shard_map/all_gather | solution.py:15
  89.1 1.5 fusion.29
  90.7 4.4 %fusion.16 = f32[4,256,128]{2,1,0:T(8,128)S(1)} fusion(f32[4,256,10]{1,2,0:T(8,128)S(1)} %copy-done.19, f32[1,10,128,64]{2,3,1,0:T(8,128)S(1)} %get-tuple-element.281, f32[1,10,128,64]{2,3,1,0:T(8,128)S(1)} %bitcast.185, f32[1,10,128,64]{2,3,1,0:T(8,128)S(1)} %get-tuple-element.288, f32[1,10,128,64]{2,3,1,0:T(8,128)S(1)} %bitcast.175, ...), kind=kOutput, calls=%fused_computation.37 | convolution fusion | flops 1008926720 | bytes 3186688 | tf_op jit(solution)/shard_map/cthp,chnp->ctn/dot_general | solution.py:40
  95.1 1.2 fusion.19
  96.4 4.4 %fusion.17 = f32[4,256,128]{2,1,0:T(8,128)S(1)} fusion(f32[4,256,10]{1,2,0:T(8,128)S(1)} %copy-done.17, f32[1,10,128,64]{2,3,1,0:T(8,128)S(1)} %bitcast.173, f32[1,10,128,64]{2,3,1,0:T(8,128)S(1)} %get-tuple-element.299, f32[1,10,128,64]{2,3,1,0:T(8,128)S(1)} %bitcast.183, f32[1,10,128,64]{2,3,1,0:T(8,128)S(1)} %get-tuple-element.300, ...), kind=kOutput, calls=%fused_computation.38 | convolution fusion | flops 1008926720 | bytes 3186688 | tf_op jit(solution)/shard_map/cshp,chnp->csn/dot_general | solution.py:40
  100.9 1.2 fusion.18
  102.1 1.1 convolution_add_fusion.1
  103.2 1.3 convolution_add_fusion
  104.5 4.0 %fusion.7 = (f32[4,256,10]{1,2,0:T(8,128)S(1)}, bf16[4,256,10,64]{1,3,2,0:T(8,128)(2,1)S(1)}) fusion(bf16[4,256,10,64]{1,0,3,2:T(4,128)(2,1)S(1)} %copy-done.11, f32[4,10,64,256]{3,2,1,0:T(8,128)S(1)} %fusion.19, f32[4,256,10]{1,2,0:T(8,128)S(1)} %copy-done.19, bf16[4,256,10,64]{1,0,3,2:T(4,128)(2,1)S(1)} %copy-done.8, f32[4,10,256]{2,1,0:T(8,128)S(1)} %copy-done.21, ...), kind=kOutput, calls=%fused_computation.22 | convolution fusion | flops 352573440 | bytes 7790592 | tf_op jit(solution)/shard_map/chts,cshp->cthp/dot_general | solution.py:59
  108.5 3.7 %fusion.6 = (f32[4,256,10]{1,2,0:T(8,128)S(1)}, bf16[4,256,10,64]{1,3,2,0:T(8,128)(2,1)S(1)}) fusion(bf16[4,256,10,64]{1,0,3,2:T(4,128)(2,1)S(1)} %copy-done.8, f32[4,10,64,256]{3,2,1,0:T(8,128)S(1)} %fusion.18, f32[4,256,10]{1,2,0:T(8,128)S(1)} %copy-done.17, f32[4,10,256]{2,1,0:T(8,128)S(1)} %copy-done.21, f32[4,256,256]{2,1,0:T(8,128)S(1)} %copy-done.12, ...), kind=kOutput, calls=%fused_computation.21 | convolution fusion | flops 352573440 | bytes 7790592 | tf_op jit(solution)/shard_map/chts,cthp->cshp/dot_general | solution.py:60
  112.4 0.2 dynamic-update-slice.1
  112.6 17.1 %all-reduce.1 = f32[40]{0:T(128)S(1)} all-reduce(f32[40]{0:T(128)S(1)} %dynamic-update-slice.1), channel_id=3, replica_groups=mesh['grp'=2,'ctx'=4,'head'=4] {'ctx'}, use_global_device_ids=true, to_apply=%add.1 | all-reduce | flops 40 | bytes 320
  130.0 1.0 copy.103
  131.0 0.3 copy.126
  131.3 1.4 copy.117
  132.8 0.6 rev.7
  133.4 2.8 %reduce-window.16 = f32[10,8,128]{2,1,0:T(8,128)S(1)} reduce-window(f32[10,8,128]{2,1,0:T(8,128)S(1)} %slice.97, f32[]{:T(128)} %constant.85.clone.1), window={size=1x1x128 pad=0_0x0_0x127_0}, to_apply=%region_12.13 | reduce-window | flops 1300480 | bytes 81924 | tf_op jit(solution)/shard_map/reduce-window.2
  136.7 0.6 rev.8
  137.3 1.0 copy.110
  138.4 0.3 copy.127
  138.6 1.4 copy.118
  140.1 0.7 broadcast_add_fusion
  140.8 23.6 %all-reduce.5.cloned.1.call-done = (f32[1024,128]{1,0:T(8,128)}, f32[1024,128]{1,0:T(8,128)}) async-done(((f32[1024,128]{1,0:T(8,128)}, f32[1024,128]{1,0:T(8,128)}), (f32[1024,128]{1,0:T(8,128)}, f32[1024,128]{1,0:T(8,128)})) %all-reduce.5.cloned.1.call-update) | async-done | bytes 1048592 | tf_op jit(solution)/shard_map/psum | solution.py:111
  164.4 1.9 %copy.194 = f32[1024,128]{1,0:T(8,128)} copy(f32[1024,128]{1,0:T(8,128)} %get-tuple-element.473) | data formatting | bytes 1048576
  166.3 0.8 copy.195
  (108 shorter events, 4.0 us)
Async XLA Ops:
  7.2 9.9 %copy-start = (bf16[1024,128]{1,0:T(8,128)(2,1)S(1)}, bf16[1024,128]{1,0:T(8,128)(2,1)}, u32[]{:S(2)}) copy-start(bf16[1024,128]{1,0:T(8,128)(2,1)} %param.13) | copy-start | bytes 786436
  7.2 4.3 %copy-start.5 = (bf16[1024,640]{1,0:T(8,128)(2,1)S(1)}, bf16[1024,640]{1,0:T(8,128)(2,1)}, u32[]{:S(2)}) copy-start(bf16[1024,640]{1,0:T(8,128)(2,1)} %param.11) | copy-start | bytes 3932164
  7.2 48.1 %all-gather.7.cloned.1.call-start = ((), (), s32[]{:S(2)}) async-start(), calls=%async_computation.1 | async-start | bytes 1638400 | tf_op jit(solution)/shard_map/all_gather | solution.py:15
  11.2 7.2 %copy-start.22 = (f32[10]{0:T(128)}, f32[10]{0:T(128)S(1)}, u32[]{:S(2)}) copy-start(f32[10]{0:T(128)S(1)} %get-tuple-element.296) | copy-start | bytes 124
  11.4 5.7 %copy-start.18 = (f32[4,256,10]{1,2,0:T(8,128)}, f32[4,256,10]{1,2,0:T(8,128)S(1)}, u32[]{:S(2)}) copy-start(f32[4,256,10]{1,2,0:T(8,128)S(1)} %copy.95) | copy-start | bytes 122884
  11.5 5.1 %copy-start.16 = (f32[4,256,10]{1,2,0:T(8,128)}, f32[4,256,10]{1,2,0:T(8,128)S(1)}, u32[]{:S(2)}) copy-start(f32[4,256,10]{1,2,0:T(8,128)S(1)} %copy.99) | copy-start | bytes 122884
  12.1 1.9 %copy-start.6 = (bf16[1024,640]{1,0:T(8,128)(2,1)S(1)}, bf16[1024,640]{1,0:T(8,128)(2,1)}, u32[]{:S(2)}) copy-start(bf16[1024,640]{1,0:T(8,128)(2,1)} %param.15) | copy-start | bytes 3932164
  14.7 1.9 %copy-start.2 = (bf16[1024,128]{1,0:T(8,128)(2,1)S(1)}, bf16[1024,128]{1,0:T(8,128)(2,1)}, u32[]{:S(2)}) copy-start(bf16[1024,128]{1,0:T(8,128)(2,1)} %param.12) | copy-start | bytes 786436
  14.7 1.9 %copy-start.7 = (bf16[4,256,10,64]{1,0,3,2:T(4,128)(2,1)S(1)}, bf16[4,256,10,64]{1,0,3,2:T(4,128)(2,1)}, u32[]{:S(2)}) copy-start(bf16[4,256,10,64]{1,0,3,2:T(4,128)(2,1)} %reshape.99) | copy-start | bytes 3932164
  16.5 1.3 copy-start.9
  18.4 1.3 copy-start.1
  18.4 2.2 %copy-start.25 = (u32[32]{0:T(128)S(1)}, u32[32]{0:T(128)}, u32[]{:S(2)}) copy-start(u32[32]{0:T(128)} %constant.94) | copy-start | bytes 388
  19.7 68.9 %all-gather.5.cloned.1.call-start = ((), (), s32[]{:S(2)}) async-start(), calls=%async_computation | async-start | bytes 1638400 | tf_op jit(solution)/shard_map/all_gather | solution.py:15
  20.4 143.9 %all-reduce.5.cloned.1.call-start = ((), (), s32[]{:S(2)}) async-start(), calls=%async_computation.2 | async-start | bytes 2097152 | tf_op jit(solution)/shard_map/psum | solution.py:111
  20.5 21.7 %copy-start.14 = (pred[256,256]{1,0:T(8,128)(4,1)}, pred[256,256]{1,0:T(8,128)(4,1)S(1)}, u32[]{:S(2)}) copy-start(pred[256,256]{1,0:T(8,128)(4,1)S(1)} %iota_compare_fusion) | copy-start | bytes 196612
  20.5 21.7 %copy-start.20 = (f32[4,10,256]{2,1,0:T(8,128)}, f32[4,10,256]{2,1,0:T(8,128)S(1)}, u32[]{:S(2)}) copy-start(f32[4,10,256]{2,1,0:T(8,128)S(1)} %copy.91) | copy-start | bytes 122884
  35.7 1.5 copy-start.10
  89.0 1.6 copy-start.11
  89.0 1.6 copy-start.19
  95.1 1.3 copy-start.8
  95.1 1.3 copy-start.17
  96.4 4.4 %copy-start.3 = (bf16[1024,128]{1,0:T(8,128)(2,1)S(1)}, bf16[1024,128]{1,0:T(8,128)(2,1)}, u32[]{:S(2)}) copy-start(bf16[1024,128]{1,0:T(8,128)(2,1)} %param.12) | copy-start | bytes 786436
  100.8 1.2 copy-start.4
  103.2 1.3 copy-start.12
  103.2 1.3 copy-start.15
  103.2 1.3 copy-start.21
  164.4 1.9 %copy-start.13 = (f32[1024,128]{1,0:T(8,128)S(1)}, f32[1024,128]{1,0:T(8,128)}, u32[]{:S(2)}) copy-start(f32[1024,128]{1,0:T(8,128)} %get-tuple-element.474) | copy-start | bytes 1572868
Sparse Core Ops, SparseCore 0:
  19.8 35.4 all-gather.6
  56.8 31.6 all-gather.4
  130.0 34.3 all-reduce.4
where the time goes:
time: 174 us
  waiting for transfers between devices  66 us (38%)
  blocking collectives  30.7 us (18%)
  matrix products  28.7 us (16%)
  local copies, waits for them, and re-layouts  23.2 us (13%)
  between operations  15 us (9%)
  other arithmetic  9.6 us (6%)
    all_gather x2, waiting for transfers between devices, entering_2(): gathered = jax.tree.map(lambda a: lax.all_gather(a, axis), part)  41.7 us
    unnamed x2, blocking collectives  30.7 us
    psum x1, waiting for transfers between devices, per_device(): lax.psum((db_full.reshape(tokens, STATE), dc_full.reshape(tokens, STATE))...  23.6 us
    dot_general x4, matrix products, exact_product(): return jnp.einsum(form, left, right, precision=lax.Precision.HIGHEST)  11.3 us
    unnamed x66, local copies, waits for them, and re-layouts  9.85 us
    another operation x6, other arithmetic  5.32 us
    dot_general x1, matrix products, per_device(): jnp.einsum('cthp,cshp->chts', dy_blocks, x_blocks, preferred_element_type...  4.98 us
    dot_general x1, matrix products, per_device(): jnp.einsum('chts,cshp->cthp', weights, x_blocks, preferred_element_type=j...  3.98 us
  transfers between devices with their start and end apart: 3, of which 3 were waited for; matrix products, arithmetic and copies ran while one was open for 13% of the time, Pallas kernels for 0%

commit v1 on v0

v1 whole, which is shorter than its diff:
```python
import functools
import math

import jax
import jax.numpy as jnp
from jax import lax
from jax.experimental import pallas as pl
from jax.experimental.pallas import tpu as pltpu
from jax.sharding import PartitionSpec as P

HEAD_DIM = 64
STATE = 128
BLOCK = 256
LANES = 128
HOP_UNITS = 7
CHUNK_UNITS = 3
LOG2E = math.log2(math.e)
F32 = jnp.float32
BF16 = jnp.bfloat16
MESH = pl.DeviceIdType.MESH


def mxu(left, right, contract, precision=None):
    return lax.dot_general(
        left, right, (contract, ((), ())), preferred_element_type=F32, precision=precision
    )


def exact(left, right, contract=((1,), (0,))):
    return mxu(left, right, contract, lax.Precision.HIGHEST)


def iota(shape, dim):
    return lax.broadcasted_iota(jnp.int32, shape, dim)


def mixer_kernel(
    ring, chips, heads, blocks,
    x_hbm, b_hbm, c_hbm, ld_ref, dy_hbm,
    y_hbm, dx_hbm, db_hbm, dc_hbm, dg_ref,
    vec, coef, ldp, runc, runr, scale, gain, scaled, pieces, states, dev, inc, out_state,
    inner, rounded_out, grads, ptotal, bal, mate_in, far_in, back_in,
    load_sem, store_sem, grad_store_sem,
    chain_send, chain_recv, mate_send, mate_recv, far_send, far_recv, back_send, back_recv,
):
    place = lax.axis_index("ctx")
    head = lax.axis_index("head")
    core = lax.rem(head, 2)
    mate = head + 1 - 2 * core
    chip = lax.div(head, 2)
    pairs = heads // 2
    width = heads * HEAD_DIM
    half = BLOCK // 2

    loads = [
        pltpu.make_async_copy(dy_hbm, vec.at[0], load_sem.at[0]),
        pltpu.make_async_copy(x_hbm, vec.at[1], load_sem.at[1]),
        pltpu.make_async_copy(c_hbm, coef.at[0], load_sem.at[2]),
        pltpu.make_async_copy(b_hbm, coef.at[1], load_sem.at[3]),
    ]
    for copy in loads:
        copy.start()

    barrier = pltpu.get_barrier_semaphore()
    pl.semaphore_signal(barrier, inc=1, device_id={"head": mate}, device_id_type=MESH)
    for hop in range(1, chips):
        pl.semaphore_signal(
            barrier, inc=1, device_id={"head": lax.rem(head + 2 * hop, 2 * chips)}, device_id_type=MESH
        )

    @pl.when(place > 0)
    def _():
        pl.semaphore_signal(barrier, inc=1, device_id={"ctx": place - 1}, device_id_type=MESH)

    @pl.when(place < ring - 1)
    def _():
        pl.semaphore_signal(barrier, inc=1, device_id={"ctx": place + 1}, device_id_type=MESH)

    ldp[...] = jnp.zeros_like(ldp)
    ldp[:, 0:heads] = ld_ref[...]
    lower = (iota((BLOCK, BLOCK), 0) >= iota((BLOCK, BLOCK), 1)).astype(F32)
    spread = (iota((LANES, width), 0) == lax.div(iota((LANES, width), 1), HEAD_DIM)).astype(F32)

    @pl.loop(0, blocks)
    def _(j):
        rows = pl.ds(pl.multiple_of(j * BLOCK, BLOCK), BLOCK)
        run = exact(lower, ldp[rows, :]) * LOG2E
        runc[j] = run
        runr[j] = run.T
        wide = exact(run, spread)
        total = wide[BLOCK - 1 :, :]
        scale[0, rows, :] = jnp.exp2(wide)
        scale[1, rows, :] = jnp.exp2(total - wide)
        gain[j] = jnp.broadcast_to(jnp.exp2(total), (8, width))

    for copy in loads:
        copy.wait()

    @pl.loop(0, 2 * blocks)
    def _(i):
        d = i // blocks
        j = i % blocks
        rows = pl.ds(pl.multiple_of(j * BLOCK, BLOCK), BLOCK)
        row = (vec[d, rows, :].astype(F32) * scale[d, rows, :]).astype(BF16)
        scaled[d, rows, :] = row
        pieces[1 - d, j] = mxu(coef[d, rows, :], row, ((0,), (0,)))

    product = gain[0, 0:1, :]
    for j in range(1, blocks):
        product = product * gain[j, 0:1, :]
    forward = pieces[0, 0]
    backward = pieces[1, blocks - 1]
    for j in range(1, blocks):
        forward = gain[j, 0:1, :] * forward + pieces[0, j]
        k = blocks - 1 - j
        backward = gain[k, 0:1, :] * backward + pieces[1, k]
    for p in range(pairs):
        lanes = slice(p * LANES, (p + 1) * LANES)
        dev[0, p] = forward[:, lanes]
        dev[1, p] = backward[:, lanes]
        gain[blocks + p, :, 0:LANES] = jnp.broadcast_to(product[:, lanes], (8, LANES))

    pl.semaphore_wait(barrier, chips + (place > 0).astype(jnp.int32) + (place < ring - 1).astype(jnp.int32))

    first = (2 * place > ring - 1).astype(jnp.int32)
    second = 1 - first

    def hops(d):
        return jnp.where(d == 0, place, ring - 1 - place)

    def chain_copy(d, p):
        target = jnp.where(d == 0, place + 1, place - 1)
        return pltpu.make_async_remote_copy(
            src_ref=out_state.at[d, p],
            dst_ref=inc.at[d, p],
            send_sem=chain_send.at[d, p],
            recv_sem=chain_recv.at[d, p],
            device_id={"ctx": jnp.clip(target, 0, ring - 1)},
            device_id_type=MESH,
        )

    def relay(d, p):
        chain_copy(d, p).wait_recv()

        @pl.when(hops(d) < ring - 1)
        def _():
            out_state[d, p] = gain[blocks + p, 0:1, 0:LANES] * inc[d, p] + dev[d, p]
            chain_copy(d, p).start()

    for d in range(2):

        @pl.when(hops(d) == 0)
        def _():
            @pl.loop(0, pairs)
            def _(p):
                inc[d, p] = jnp.zeros((STATE, LANES), F32)
                if ring > 1:
                    out_state[d, p] = dev[d, p]
                    chain_copy(d, p).start()

    def tick(unit):
        for d in (first, second):
            since = unit - HOP_UNITS * hops(d)
            p = jnp.maximum(since, 0) // CHUNK_UNITS

            @pl.when((hops(d) > 0) & (since >= 0) & (since == p * CHUNK_UNITS) & (p < pairs))
            def _():
                relay(d, p)

    last_unit = HOP_UNITS * (ring - 1) + CHUNK_UNITS * (pairs - 1) + 1

    low_lanes = iota((1, LANES), 1) < HEAD_DIM

    @pl.loop(0, blocks)
    def _(j):
        rows = pl.ds(pl.multiple_of(j * BLOCK, BLOCK), BLOCK)
        causal = iota((BLOCK, BLOCK), 0) >= iota((BLOCK, BLOCK), 1)
        scores = jnp.where(causal, mxu(coef[0, rows, :], coef[1, rows, :], ((1,), (1,))), 0.0)
        ptotal[0] = scores
        for p in range(pairs):
            lanes = slice(p * LANES, (p + 1) * LANES)
            x2 = vec[1, rows, lanes]
            dy2 = vec[0, rows, lanes]
            y2 = None
            for k in range(2):
                h = 2 * p + k
                mine = low_lanes if k == 0 else jnp.logical_not(low_lanes)
                xm = jnp.where(mine, x2, jnp.zeros_like(x2))
                dym = jnp.where(mine, dy2, jnp.zeros_like(dy2))
                decays = jnp.exp2(jnp.minimum(runc[j, :, h : h + 1] - runr[j, h : h + 1, :], 0.0))
                weights = (ptotal[0] * decays).astype(BF16)
                pair = mxu(dy2, xm, ((1,), (1,))) * decays
                if h == 0:
                    ptotal[1] = pair
                else:
                    ptotal[1] += pair
                y_add = mxu(weights, xm, ((1,), (0,)))
                dx_add = mxu(weights, dym, ((0,), (0,)))
                y2 = y_add if y2 is None else y2 + y_add
                dx2 = dx_add if k == 0 else dx2 + dx_add
            inner[0, rows, lanes] = y2
            inner[1, rows, lanes] = dx2
            tick(j * pairs + p)
        both = jnp.where(causal, ptotal[1], 0.0).astype(BF16)
        grads[0, rows, :] = mxu(both, coef[1, rows, :], ((1,), (0,)))
        grads[1, rows, :] = mxu(both, coef[0, rows, :], ((0,), (0,)))

    own_rows = core * half
    mate_rows = half - own_rows

    def piece_of(j, at):
        return pl.ds(pl.multiple_of(j * BLOCK + at, half), half)

    def mate_copy(d, j):
        return pltpu.make_async_remote_copy(
            src_ref=grads.at[d, piece_of(j, mate_rows), :],
            dst_ref=mate_in.at[d, j],
            send_sem=mate_send.at[d, j],
            recv_sem=mate_recv.at[d, j],
            device_id={"head": mate},
            device_id_type=MESH,
        )

    def far_copy(d, j, hop):
        return pltpu.make_async_remote_copy(
            src_ref=mate_in.at[d, j],
            dst_ref=far_in.at[d, j, chip],
            send_sem=far_send.at[d, j, hop],
            recv_sem=far_recv.at[d, j, chip],
            device_id={"head": lax.rem(head + 2 * hop, 2 * chips)},
            device_id_type=MESH,
        )

    def far_arrival(d, j, hop):
        source = lax.rem(chip + chips - hop, chips)
        return pltpu.make_async_remote_copy(
            src_ref=mate_in.at[d, j],
            dst_ref=far_in.at[d, j, source],
            send_sem=far_send.at[d, j, hop],
            recv_sem=far_recv.at[d, j, source],
            device_id={"head": lax.rem(head + 2 * hop, 2 * chips)},
            device_id_type=MESH,
        )

    def back_copy(d, j):
        return pltpu.make_async_remote_copy(
            src_ref=grads.at[d, piece_of(j, own_rows), :],
            dst_ref=back_in.at[d, j],
            send_sem=back_send.at[d, j],
            recv_sem=back_recv.at[d, j],
            device_id={"head": mate},
            device_id_type=MESH,
        )

    def local_sum(d, j):
        mate_copy(d, j).wait_recv()
        total = mate_in[d, j] + grads[d, piece_of(j, own_rows), :]
        mate_in[d, j] = total
        far_in[d, j, chip] = total
        for hop in range(1, chips):
            far_copy(d, j, hop).start()

    def far_sum(d, j):
        for hop in range(1, chips):
            far_arrival(d, j, hop).wait_recv()
        total = far_in[d, j, 0]
        for source in range(1, chips):
            total = total + far_in[d, j, source]
        grads[d, piece_of(j, own_rows), :] = total
        back_copy(d, j).start()

    def order(d, i):
        return jnp.where(d == 0, i, blocks - 1 - i)

    def outer(d, start, is_second):
        state = jnp.concatenate([inc[d, p] for p in range(pairs)], axis=1)
        states[d, blocks] = state

        @pl.loop(0, blocks)
        def _(i):
            j = order(d, i)
            rows = pl.ds(pl.multiple_of(j * BLOCK, BLOCK), BLOCK)
            now = states[d, blocks]
            states[d, j] = now
            states[d, blocks] = gain[j, 0:1, :] * now + pieces[d, j]
            held = now.astype(BF16)
            grads[d, rows, :] += mxu(scaled[d, rows, :], held, ((1,), (1,)))
            mate_copy(d, j).start()
            full = inner[d, rows, :] + scale[d, rows, :] * mxu(coef[d, rows, :], held, ((1,), (0,)))
            rounded_out[d, rows, :] = full.astype(BF16)
            term = vec[d, rows, :].astype(F32) * full
            high = term.astype(BF16)
            low = (term - high.astype(F32)).astype(BF16)
            gather = spread.astype(BF16)
            summed = mxu(high, gather, ((1,), (1,))) + mxu(low, gather, ((1,), (1,)))
            summed = jnp.where(d == 0, summed, -summed)
            if is_second:
                bal[rows, :] += summed
            else:
                bal[rows, :] = summed
                tick(start + i)

            @pl.when(i > 0)
            def _():
                local_sum(d, order(d, i - 1))

        local_sum(d, order(d, blocks - 1))

        @pl.when(d == 0)
        def _():
            pltpu.make_async_copy(rounded_out.at[0], y_hbm, store_sem.at[0]).start()

        @pl.when(d == 1)
        def _():
            pltpu.make_async_copy(rounded_out.at[1], dx_hbm, store_sem.at[1]).start()

    units = blocks * pairs

    @pl.loop(units, jnp.maximum(units, HOP_UNITS * hops(first) + CHUNK_UNITS * (pairs - 1) + 1))
    def _(u):
        tick(u)

    start = jnp.maximum(units, HOP_UNITS * hops(first) + CHUNK_UNITS * (pairs - 1) + 1)
    outer(first, start, False)

    @pl.loop(start + blocks, jnp.maximum(start + blocks, last_unit))
    def _(u):
        tick(u)

    @pl.loop(0, blocks)
    def _(i):
        far_sum(first, order(first, i))

    outer(second, 0, True)

    gather = spread

    @pl.loop(0, blocks)
    def _(j):
        rows = pl.ds(pl.multiple_of(j * BLOCK, BLOCK), BLOCK)
        joint = jnp.sum(states[0, j + 1] * states[1, j], axis=0, keepdims=True)
        later = exact(jnp.broadcast_to(joint, (8, width)), gather, ((1,), (1,)))[0:1, :]
        suffix = exact(lower, bal[rows, :], ((0,), (0,))) + later
        dg_ref[rows, :] = suffix[:, 0:heads]

    @pl.loop(0, blocks)
    def _(i):
        far_sum(second, order(second, i))

    def own_store(d, j):
        target = dc_hbm if d == 0 else db_hbm
        rows = piece_of(j, own_rows)
        return pltpu.make_async_copy(grads.at[d, rows, :], target.at[rows, :], grad_store_sem.at[d, j, 0])

    def mate_store(d, j):
        target = dc_hbm if d == 0 else db_hbm
        rows = piece_of(j, mate_rows)
        return pltpu.make_async_copy(back_in.at[d, j], target.at[rows, :], grad_store_sem.at[d, j, 1])

    @pl.loop(0, blocks)
    def _(j):
        for d in range(2):
            own_store(d, j).start()

    @pl.loop(0, blocks)
    def _(j):
        for d in range(2):
            back_copy(d, j).wait_recv()
            mate_store(d, j).start()

    @pl.loop(0, blocks)
    def _(j):
        for d in range(2):
            own_store(d, j).wait()
            mate_store(d, j).wait()
            mate_copy(d, j).wait_send()
            back_copy(d, j).wait_send()
            for hop in range(1, chips):
                far_copy(d, j, hop).wait_send()

    pltpu.make_async_copy(rounded_out.at[0], y_hbm, store_sem.at[0]).wait()
    pltpu.make_async_copy(rounded_out.at[1], dx_hbm, store_sem.at[1]).wait()

    for d in range(2):

        @pl.when(hops(d) < ring - 1)
        def _():
            @pl.loop(0, pairs)
            def _(p):
                chain_copy(d, p).wait_send()


def per_device(ring, chips, inputs, write_coeffs, read_coeffs, log_decay, out_grad):
    tokens = inputs.shape[0]
    real = log_decay.shape[1]
    heads = real + real % 2
    if heads > real:
        extra = ((0, 0), (0, (heads - real) * HEAD_DIM))
        inputs = jnp.pad(inputs, extra)
        out_grad = jnp.pad(out_grad, extra)
        log_decay = jnp.pad(log_decay, ((0, 0), (0, heads - real)))
    width = heads * HEAD_DIM
    blocks = tokens // BLOCK
    pairs = heads // 2
    half = BLOCK // 2
    any_spec = pl.BlockSpec(memory_space=pl.ANY)
    vmem_spec = pl.BlockSpec(memory_space=pltpu.VMEM)
    dma = pltpu.SemaphoreType.DMA
    y, dx, db, dc, dg = pl.pallas_call(
        functools.partial(mixer_kernel, ring, chips, heads, blocks),
        out_shape=(
            jax.ShapeDtypeStruct((tokens, width), BF16),
            jax.ShapeDtypeStruct((tokens, width), BF16),
            jax.ShapeDtypeStruct((tokens, STATE), F32),
            jax.ShapeDtypeStruct((tokens, STATE), F32),
            jax.ShapeDtypeStruct((tokens, heads), F32),
        ),
        in_specs=[any_spec, any_spec, any_spec, vmem_spec, any_spec],
        out_specs=(any_spec, any_spec, any_spec, any_spec, vmem_spec),
        scratch_shapes=[
            pltpu.VMEM((2, tokens, width), BF16),
            pltpu.VMEM((2, tokens, STATE), BF16),
            pltpu.VMEM((tokens, LANES), F32),
            pltpu.VMEM((blocks, BLOCK, LANES), F32),
            pltpu.VMEM((blocks, LANES, BLOCK), F32),
            pltpu.VMEM((2, tokens, width), F32),
            pltpu.VMEM((blocks + pairs, 8, width), F32),
            pltpu.VMEM((2, tokens, width), BF16),
            pltpu.VMEM((2, blocks, STATE, width), F32),
            pltpu.VMEM((2, blocks + 1, STATE, width), F32),
            pltpu.VMEM((2, pairs, STATE, LANES), F32),
            pltpu.VMEM((2, pairs, STATE, LANES), F32),
            pltpu.VMEM((2, pairs, STATE, LANES), F32),
            pltpu.VMEM((2, tokens, width), F32),
            pltpu.VMEM((2, tokens, width), BF16),
            pltpu.VMEM((2, tokens, STATE), F32),
            pltpu.VMEM((2, BLOCK, BLOCK), F32),
            pltpu.VMEM((tokens, LANES), F32),
            pltpu.VMEM((2, blocks, half, STATE), F32),
            pltpu.VMEM((2, blocks, chips, half, STATE), F32),
            pltpu.VMEM((2, blocks, half, STATE), F32),
            dma((4,)),
            dma((2,)),
            dma((2, blocks, 2)),
            dma((2, pairs)),
            dma((2, pairs)),
            dma((2, blocks)),
            dma((2, blocks)),
            dma((2, blocks, chips)),
            dma((2, blocks, chips)),
            dma((2, blocks)),
            dma((2, blocks)),
        ],
        compiler_params=pltpu.CompilerParams(
            collective_id=0, has_side_effects=True, vmem_limit_bytes=56 * 1024 * 1024
        ),
    )(inputs, write_coeffs, read_coeffs, log_decay, out_grad)
    if heads > real:
        y = y[:, : real * HEAD_DIM]
        dx = dx[:, : real * HEAD_DIM]
        dg = dg[:, :real]
    return (y, dx, db, dc, dg)


def solution(mesh):
    in_specs = (
        P(("grp", "ctx"), "head"),
        P(("grp", "ctx"), None),
        P(("grp", "ctx"), None),
        P(("grp", "ctx"), "head"),
        P(("grp", "ctx"), "head"),
    )
    out_specs = (
        P(("grp", "ctx"), "head"),
        P(("grp", "ctx"), "head"),
        P(("grp", "ctx"), None),
        P(("grp", "ctx"), None),
        P(("grp", "ctx"), "head"),
    )
    return jax.shard_map(
        functools.partial(per_device, mesh.shape["ctx"], mesh.shape["head"] // 2),
        mesh=mesh,
        in_specs=in_specs,
        out_specs=out_specs,
        check_vma=False,
    )
```

time: 174 us -> 54.2 us (0.31)
  waiting for transfers between devices: 66 us -> 0 us
  Pallas kernels: 0 us -> 43.4 us
  blocking collectives: 30.7 us -> 0 us
  matrix products: 28.7 us -> 0 us
  between operations: 15 us -> 0.64 us
  local copies, waits for them, and re-layouts: 23.2 us -> 9.27 us
  other arithmetic: 9.6 us -> 0 us
    pallas_call x0 -> x1, Pallas kernels: none -> 43.4 us  [per_device(): pl.pallas_call(functools.partial(mixer_kernel, ring, chips, heads, blocks...]
    all_gather x2 -> x0, waiting for transfers between devices: 41.7 us -> none  [entering_2(): gathered = jax.tree.map(lambda a: lax.all_gather(a, axis), part)]
    unnamed x2 -> x0, blocking collectives: 30.7 us -> none
    dot_general x12 -> x0, matrix products: 28.7 us -> none  [the longest x4 11.3 us: exact_product(): return jnp.einsum(form, left, right, precision=lax.Precision.HIGHEST)]
    psum x1 -> x0, waiting for transfers between devices: 23.6 us -> none  [per_device(): lax.psum((db_full.reshape(tokens, STATE), dc_full.reshape(tokens, STATE))...]
    another operation x7 -> x0, other arithmetic: 6.86 us -> none
    reshape x5 -> x0, local copies, waits for them, and re-layouts: 4.72 us -> none  [the longest x1 1.86 us: per_device(): dy_blocks = out_grad.reshape(blocks, BLOCK, heads, HEAD_DIM)]
    dynamic_slice x6 -> x0, local copies, waits for them, and re-layouts: 3.71 us -> none  [one(): lax.dynamic_index_in_dim(a, source, 0, False)]
  transfers between devices with their start and end apart: 3 -> 0, of which waited for: 3 -> 0; matrix products, arithmetic and copies ran while one was open for 13% -> 0% of each run, Pallas kernels for 0% -> 0%
where the time goes in v1:
time: 54.2 us; the launch traced here: 53.3 us
  Pallas kernels  43.4 us (80%)
  local copies, waits for them, and re-layouts  9.27 us (17%)
  between operations  0.64 us (1%)
    pallas_call x1, Pallas kernels, per_device(): pl.pallas_call(functools.partial(mixer_kernel, ring, chips, heads, blocks...  43.4 us
    unnamed x11, local copies, waits for them, and re-layouts  7.41 us
    pallas_call x1, local copies, waits for them, and re-layouts, per_device(): pl.pallas_call(functools.partial(mixer_kernel, ring, chips, heads, blocks...  1.86 us

profile of v1, /device:TPU:0, one launch (start us, length us, event | category | flops | bytes accessed | tf_op | source)
XLA Modules:
  0.0 53.3 jit_solution(5889120974287403424)
XLA Ops:
  0.6 1.9 %copy.10.ld_ref = f32[1024,10]{1,0:T(8,128)} copy(f32[1024,10]{0,1:T(8,128)} %param.8) | data formatting | bytes 81920 | tf_op args[3]
  2.5 43.4 %shard_map.92 = (bf16[1024,640]{1,0:T(8,128)(2,1)}, bf16[1024,640]{1,0:T(8,128)(2,1)}, f32[1024,128]{1,0:T(8,128)}, f32[1024,128]{1,0:T(8,128)}, f32[1024,10]{1,0:T(8,128)}) custom-call(bf16[1024,640]{1,0:T(8,128)(2,1)} %x_hbm.1, bf16[1024,128]{1,0:T(8,128)(2,1)} %b_hbm.1, bf16[1024,128]{1,0:T(8,128)(2,1)} %c_hbm.1, f32[1024,10]{1,0:T(8,128)} %copy.10.ld_ref, ...), custom_call_target="tpu_custom_call" | custom-call | tf_op jit(solution)/shard_map/pallas_call | solution.py:409
  45.9 1.9 %copy.11 = f32[1024,10]{0,1:T(8,128)} copy(f32[1024,10]{1,0:T(8,128)} %get-tuple-element.9) | data formatting | bytes 81920 | tf_op jit(solution)/shard_map/pallas_call | solution.py:409
  47.8 0.0 copy-start
  47.8 2.6 %copy.16 = bf16[1024,640]{1,0:T(8,128)(2,1)} copy(bf16[1024,640]{1,0:T(8,128)(2,1)} %get-tuple-element.15) | data formatting | bytes 2621440
  50.3 0.0 copy-done
  50.4 0.0 copy-start.2
  50.4 0.0 copy-start.1
  50.4 1.1 %copy.17 = bf16[1024,640]{1,0:T(8,128)(2,1)} copy(bf16[1024,640]{1,0:T(8,128)(2,1)S(1)} %copy-done) | data formatting | bytes 2621440
  51.4 0.3 copy-done.2
  51.7 0.8 %copy.18 = f32[1024,128]{1,0:T(8,128)} copy(f32[1024,128]{1,0:T(8,128)S(1)} %copy-done.2) | data formatting | bytes 1048576
  52.5 0.0 copy-done.1
  52.5 0.8 %copy.19 = f32[1024,128]{1,0:T(8,128)} copy(f32[1024,128]{1,0:T(8,128)S(1)} %copy-done.1) | data formatting | bytes 1048576
Async XLA Ops:
  47.8 2.6 %copy-start = (bf16[1024,640]{1,0:T(8,128)(2,1)S(1)}, bf16[1024,640]{1,0:T(8,128)(2,1)}, u32[]{:S(2)}) copy-start(bf16[1024,640]{1,0:T(8,128)(2,1)} %get-tuple-element.16) | copy-start | bytes 3932164
  50.4 1.4 %copy-start.2 = (f32[1024,128]{1,0:T(8,128)S(1)}, f32[1024,128]{1,0:T(8,128)}, u32[]{:S(2)}) copy-start(f32[1024,128]{1,0:T(8,128)} %get-tuple-element.17) | copy-start | bytes 1572868
  50.4 2.2 %copy-start.1 = (f32[1024,128]{1,0:T(8,128)S(1)}, f32[1024,128]{1,0:T(8,128)}, u32[]{:S(2)}) copy-start(f32[1024,128]{1,0:T(8,128)} %get-tuple-element.18) | copy-start | bytes 1572868

commit v2 on v1

--- a/solution.py
+++ b/solution.py
@@ -26,8 +26,12 @@
     )
 
 
-def exact(left, right, contract=((1,), (0,))):
-    return mxu(left, right, contract, lax.Precision.HIGHEST)
+def thirds(values):
+    high = values.astype(BF16)
+    rest = values - high.astype(F32)
+    middle = rest.astype(BF16)
+    low = (rest - middle.astype(F32)).astype(BF16)
+    return jnp.concatenate([high, middle, low], axis=0)
 
 
 def iota(shape, dim):
@@ -38,7 +42,7 @@
     ring, chips, heads, blocks,
     x_hbm, b_hbm, c_hbm, ld_ref, dy_hbm,
     y_hbm, dx_hbm, db_hbm, dc_hbm, dg_ref,
-    vec, coef, ldp, runc, runr, scale, gain, scaled, pieces, states, dev, inc, out_state,
+    vec, coef, ldp, runc, runr, scale, gain, scaled, pieces, states, states_held, dev, inc, out_state,
     inner, rounded_out, grads, ptotal, bal, mate_in, far_in, back_in,
     load_sem, store_sem, grad_store_sem,
     chain_send, chain_recv, mate_send, mate_recv, far_send, far_recv, back_send, back_recv,
@@ -76,49 +80,53 @@
     def _():
         pl.semaphore_signal(barrier, inc=1, device_id={"ctx": place + 1}, device_id_type=MESH)
 
+    slots = ldp.shape[0]
     ldp[...] = jnp.zeros_like(ldp)
-    ldp[:, 0:heads] = ld_ref[...]
-    lower = (iota((BLOCK, BLOCK), 0) >= iota((BLOCK, BLOCK), 1)).astype(F32)
-    spread = (iota((LANES, width), 0) == lax.div(iota((LANES, width), 1), HEAD_DIM)).astype(F32)
-
-    @pl.loop(0, blocks)
-    def _(j):
-        rows = pl.ds(pl.multiple_of(j * BLOCK, BLOCK), BLOCK)
-        run = exact(lower, ldp[rows, :]) * LOG2E
-        runc[j] = run
-        runr[j] = run.T
-        wide = exact(run, spread)
-        total = wide[BLOCK - 1 :, :]
-        scale[0, rows, :] = jnp.exp2(wide)
-        scale[1, rows, :] = jnp.exp2(total - wide)
-        gain[j] = jnp.broadcast_to(jnp.exp2(total), (8, width))
+    ldp[0:heads, :] = ld_ref[...]
+    upper = (iota((BLOCK, BLOCK), 0) <= iota((BLOCK, BLOCK), 1)).astype(F32).astype(BF16)
+    spread = (iota((slots, width), 0) == lax.div(iota((slots, width), 1), HEAD_DIM)).astype(F32)
+    spread3 = jnp.concatenate([spread] * 3, axis=0).astype(BF16)
+    gather = spread.astype(BF16)
+
+    def joined(left3, right):
+        three = mxu(left3, right, ((1,), (0,)))
+        return three[0:slots] + three[slots : 2 * slots] + three[2 * slots :]
+
+    for j in range(blocks):
+        rows = slice(j * BLOCK, (j + 1) * BLOCK)
+        run = joined(thirds(ldp[:, rows]), upper) * LOG2E
+        runr[j] = run
+        runc[j] = jnp.concatenate([run, jnp.zeros((LANES - slots, BLOCK), F32)], axis=0).T
+        grow = mxu(thirds(jnp.exp2(run)), spread3, ((0,), (0,)))
+        scale[0, rows, :] = grow
+        scale[1, rows, :] = mxu(
+            thirds(jnp.exp2(run[:, BLOCK - 1 :] - run)), spread3, ((0,), (0,))
+        )
+        gain[j] = jnp.broadcast_to(grow[BLOCK - 1 :, :], (8, width))
 
     for copy in loads:
         copy.wait()
 
-    @pl.loop(0, 2 * blocks)
-    def _(i):
-        d = i // blocks
-        j = i % blocks
-        rows = pl.ds(pl.multiple_of(j * BLOCK, BLOCK), BLOCK)
-        row = (vec[d, rows, :].astype(F32) * scale[d, rows, :]).astype(BF16)
-        scaled[d, rows, :] = row
-        pieces[1 - d, j] = mxu(coef[d, rows, :], row, ((0,), (0,)))
-
-    product = gain[0, 0:1, :]
-    for j in range(1, blocks):
-        product = product * gain[j, 0:1, :]
-    forward = pieces[0, 0]
-    backward = pieces[1, blocks - 1]
-    for j in range(1, blocks):
-        forward = gain[j, 0:1, :] * forward + pieces[0, j]
-        k = blocks - 1 - j
-        backward = gain[k, 0:1, :] * backward + pieces[1, k]
+    for j in range(blocks):
+        for d in range(2):
+            rows = slice(j * BLOCK, (j + 1) * BLOCK)
+            row = (vec[d, rows, :].astype(F32) * scale[d, rows, :]).astype(BF16)
+            scaled[d, rows, :] = row
+            pieces[1 - d, j] = mxu(coef[d, rows, :], row, ((0,), (0,)))
+
     for p in range(pairs):
         lanes = slice(p * LANES, (p + 1) * LANES)
-        dev[0, p] = forward[:, lanes]
-        dev[1, p] = backward[:, lanes]
-        gain[blocks + p, :, 0:LANES] = jnp.broadcast_to(product[:, lanes], (8, LANES))
+        product = gain[0, 0:1, lanes]
+        forward = pieces[0, 0, :, lanes]
+        backward = pieces[1, blocks - 1, :, lanes]
+        for j in range(1, blocks):
+            product = product * gain[j, 0:1, lanes]
+            forward = gain[j, 0:1, lanes] * forward + pieces[0, j, :, lanes]
+            k = blocks - 1 - j
+            backward = gain[k, 0:1, lanes] * backward + pieces[1, k, :, lanes]
+        dev[0, p] = forward
+        dev[1, p] = backward
+        gain[blocks + p, :, 0:LANES] = jnp.broadcast_to(product, (8, LANES))
 
     pl.semaphore_wait(barrier, chips + (place > 0).astype(jnp.int32) + (place < ring - 1).astype(jnp.int32))
 
@@ -272,9 +280,8 @@
     def order(d, i):
         return jnp.where(d == 0, i, blocks - 1 - i)
 
-    def outer(d, start, is_second):
-        state = jnp.concatenate([inc[d, p] for p in range(pairs)], axis=1)
-        states[d, blocks] = state
+    def outer_grads(d, start, ticking):
+        states[d, blocks] = jnp.concatenate([inc[d, p] for p in range(pairs)], axis=1)
 
         @pl.loop(0, blocks)
         def _(i):
@@ -284,27 +291,36 @@
             states[d, j] = now
             states[d, blocks] = gain[j, 0:1, :] * now + pieces[d, j]
             held = now.astype(BF16)
+            states_held[d, j] = held
             grads[d, rows, :] += mxu(scaled[d, rows, :], held, ((1,), (1,)))
             mate_copy(d, j).start()
+            if ticking:
+                tick(start + i)
+
+            @pl.when(i > 0)
+            def _():
+                local_sum(d, order(d, i - 1))
+
+        local_sum(d, order(d, blocks - 1))
+
+    def outer_rows(d, start, ticking):
+        @pl.loop(0, blocks)
+        def _(i):
+            j = order(d, i)
+            rows = pl.ds(pl.multiple_of(j * BLOCK, BLOCK), BLOCK)
+            held = states_held[d, j]
             full = inner[d, rows, :] + scale[d, rows, :] * mxu(coef[d, rows, :], held, ((1,), (0,)))
             rounded_out[d, rows, :] = full.astype(BF16)
             term = vec[d, rows, :].astype(F32) * full
             high = term.astype(BF16)
             low = (term - high.astype(F32)).astype(BF16)
-            gather = spread.astype(BF16)
-            summed = mxu(high, gather, ((1,), (1,))) + mxu(low, gather, ((1,), (1,)))
+            summed = mxu(gather, high, ((1,), (1,))) + mxu(gather, low, ((1,), (1,)))
             summed = jnp.where(d == 0, summed, -summed)
-            if is_second:
-                bal[rows, :] += summed
+            if ticking:
+                bal[j] = summed
+                tick(start + i)
             else:
-                bal[rows, :] = summed
-                tick(start + i)
-
-            @pl.when(i > 0)
-            def _():
-                local_sum(d, order(d, i - 1))
-
-        local_sum(d, order(d, blocks - 1))
+                bal[j] += summed
 
         @pl.when(d == 0)
         def _():
@@ -321,27 +337,28 @@
         tick(u)
 
     start = jnp.maximum(units, HOP_UNITS * hops(first) + CHUNK_UNITS * (pairs - 1) + 1)
-    outer(first, start, False)
-
-    @pl.loop(start + blocks, jnp.maximum(start + blocks, last_unit))
+    outer_grads(first, start, True)
+    outer_rows(first, start + blocks, True)
+    start = start + 2 * blocks
+
+    @pl.loop(start, jnp.maximum(start, last_unit))
     def _(u):
         tick(u)
+
+    outer_grads(second, 0, False)
 
     @pl.loop(0, blocks)
     def _(i):
         far_sum(first, order(first, i))
 
-    outer(second, 0, True)
-
-    gather = spread
-
-    @pl.loop(0, blocks)
-    def _(j):
-        rows = pl.ds(pl.multiple_of(j * BLOCK, BLOCK), BLOCK)
+    outer_rows(second, 0, False)
+
+    for j in range(blocks):
         joint = jnp.sum(states[0, j + 1] * states[1, j], axis=0, keepdims=True)
-        later = exact(jnp.broadcast_to(joint, (8, width)), gather, ((1,), (1,)))[0:1, :]
-        suffix = exact(lower, bal[rows, :], ((0,), (0,))) + later
-        dg_ref[rows, :] = suffix[:, 0:heads]
+        later = jnp.sum(spread * joint, axis=1, keepdims=True)
+        lower = (iota((BLOCK, BLOCK), 0) >= iota((BLOCK, BLOCK), 1)).astype(F32).astype(BF16)
+        suffix = joined(thirds(bal[j]), lower) + later
+        dg_ref[:, j * BLOCK : (j + 1) * BLOCK] = suffix[0:heads, :]
 
     @pl.loop(0, blocks)
     def _(i):
@@ -403,6 +420,7 @@
     blocks = tokens // BLOCK
     pairs = heads // 2
     half = BLOCK // 2
+    slots = -(-heads // 16) * 16
     any_spec = pl.BlockSpec(memory_space=pl.ANY)
     vmem_spec = pl.BlockSpec(memory_space=pltpu.VMEM)
     dma = pltpu.SemaphoreType.DMA
@@ -413,21 +431,22 @@
             jax.ShapeDtypeStruct((tokens, width), BF16),
             jax.ShapeDtypeStruct((tokens, STATE), F32),
             jax.ShapeDtypeStruct((tokens, STATE), F32),
-            jax.ShapeDtypeStruct((tokens, heads), F32),
+            jax.ShapeDtypeStruct((heads, tokens), F32),
         ),
         in_specs=[any_spec, any_spec, any_spec, vmem_spec, any_spec],
         out_specs=(any_spec, any_spec, any_spec, any_spec, vmem_spec),
         scratch_shapes=[
             pltpu.VMEM((2, tokens, width), BF16),
             pltpu.VMEM((2, tokens, STATE), BF16),
-            pltpu.VMEM((tokens, LANES), F32),
+            pltpu.VMEM((slots, tokens), F32),
             pltpu.VMEM((blocks, BLOCK, LANES), F32),
-            pltpu.VMEM((blocks, LANES, BLOCK), F32),
+            pltpu.VMEM((blocks, slots, BLOCK), F32),
             pltpu.VMEM((2, tokens, width), F32),
             pltpu.VMEM((blocks + pairs, 8, width), F32),
             pltpu.VMEM((2, tokens, width), BF16),
             pltpu.VMEM((2, blocks, STATE, width), F32),
             pltpu.VMEM((2, blocks + 1, STATE, width), F32),
+            pltpu.VMEM((2, blocks, STATE, width), BF16),
             pltpu.VMEM((2, pairs, STATE, LANES), F32),
             pltpu.VMEM((2, pairs, STATE, LANES), F32),
             pltpu.VMEM((2, pairs, STATE, LANES), F32),
@@ -435,7 +454,7 @@
             pltpu.VMEM((2, tokens, width), BF16),
             pltpu.VMEM((2, tokens, STATE), F32),
             pltpu.VMEM((2, BLOCK, BLOCK), F32),
-            pltpu.VMEM((tokens, LANES), F32),
+            pltpu.VMEM((blocks, slots, BLOCK), F32),
             pltpu.VMEM((2, blocks, half, STATE), F32),
             pltpu.VMEM((2, blocks, chips, half, STATE), F32),
             pltpu.VMEM((2, blocks, half, STATE), F32),
@@ -454,7 +473,8 @@
         compiler_params=pltpu.CompilerParams(
             collective_id=0, has_side_effects=True, vmem_limit_bytes=56 * 1024 * 1024
         ),
-    )(inputs, write_coeffs, read_coeffs, log_decay, out_grad)
+    )(inputs, write_coeffs, read_coeffs, log_decay.T, out_grad)
+    dg = dg.T
     if heads > real:
         y = y[:, : real * HEAD_DIM]
         dx = dx[:, : real * HEAD_DIM]

time: 54.2 us -> 44.7 us (0.82); the launches traced: 53.3 us -> 44.5 us
  Pallas kernels: 43.4 us -> 37.6 us
  local copies, waits for them, and re-layouts: 9.27 us -> 6.18 us
    pallas_call x1, Pallas kernels: 43.4 us -> 37.6 us  [per_device(): pl.pallas_call(functools.partial(mixer_kernel, ring, chips, heads, blocks...]
    pallas_call x1 -> x0, local copies, waits for them, and re-layouts: 1.86 us -> none  [per_device(): pl.pallas_call(functools.partial(mixer_kernel, ring, chips, heads, blocks...]
    unnamed x11 -> x13, local copies, waits for them, and re-layouts: 7.41 us -> 6.18 us
where the time goes in v2:
time: 44.7 us; the launch traced here: 44.5 us
  Pallas kernels  37.6 us (84%)
  local copies, waits for them, and re-layouts  6.18 us (14%)
  between operations  0.65 us (1%)
    pallas_call x1, Pallas kernels, per_device(): pl.pallas_call(functools.partial(mixer_kernel, ring, chips, heads, blocks...  37.6 us
    unnamed x13, local copies, waits for them, and re-layouts  6.18 us

profile of v2, /device:TPU:0, one launch (start us, length us, event | category | flops | bytes accessed | tf_op | source)
XLA Modules:
  0.0 44.5 jit_solution(5734289548232786860)
XLA Ops:
  0.6 37.6 %shard_map.92 = (bf16[1024,640]{1,0:T(8,128)(2,1)}, bf16[1024,640]{1,0:T(8,128)(2,1)}, f32[1024,128]{1,0:T(8,128)}, f32[1024,128]{1,0:T(8,128)}, f32[10,1024]{1,0:T(8,128)}) custom-call(bf16[1024,640]{1,0:T(8,128)(2,1)} %x_hbm.1, bf16[1024,128]{1,0:T(8,128)(2,1)} %b_hbm.1, bf16[1024,128]{1,0:T(8,128)(2,1)} %c_hbm.1, f32[10,1024]{1,0:T(8,128)} %bitcast.2, ...), custom_call_target="tpu_custom_call" | custom-call | tf_op jit(solution)/shard_map/pallas_call | solution.py:427
  38.3 0.0 copy-start
  38.3 2.6 %copy.15 = bf16[1024,640]{1,0:T(8,128)(2,1)} copy(bf16[1024,640]{1,0:T(8,128)(2,1)} %get-tuple-element.20) | data formatting | bytes 2621440
  40.9 0.0 copy-done
  40.9 0.0 copy-start.2
  40.9 0.0 copy-start.1
  40.9 1.1 %copy.16 = bf16[1024,640]{1,0:T(8,128)(2,1)} copy(bf16[1024,640]{1,0:T(8,128)(2,1)S(1)} %copy-done) | data formatting | bytes 2621440
  41.9 0.3 copy-done.2
  42.3 0.0 copy-start.3
  42.3 0.8 %copy.17 = f32[1024,128]{1,0:T(8,128)} copy(f32[1024,128]{1,0:T(8,128)S(1)} %copy-done.2) | data formatting | bytes 1048576
  43.0 0.0 copy-done.1
  43.1 0.8 %copy.18 = f32[1024,128]{1,0:T(8,128)} copy(f32[1024,128]{1,0:T(8,128)S(1)} %copy-done.1) | data formatting | bytes 1048576
  43.8 0.0 copy-done.3
  43.8 0.6 %copy.19 = f32[1024,10]{0,1:T(8,128)} copy(f32[1024,10]{0,1:T(8,128)S(1)} %bitcast.3) | data formatting | bytes 81920
Async XLA Ops:
  38.3 2.6 %copy-start = (bf16[1024,640]{1,0:T(8,128)(2,1)S(1)}, bf16[1024,640]{1,0:T(8,128)(2,1)}, u32[]{:S(2)}) copy-start(bf16[1024,640]{1,0:T(8,128)(2,1)} %get-tuple-element.21) | copy-start | bytes 3932164
  40.9 1.4 %copy-start.2 = (f32[1024,128]{1,0:T(8,128)S(1)}, f32[1024,128]{1,0:T(8,128)}, u32[]{:S(2)}) copy-start(f32[1024,128]{1,0:T(8,128)} %get-tuple-element.22) | copy-start | bytes 1572868
  40.9 2.2 %copy-start.1 = (f32[1024,128]{1,0:T(8,128)S(1)}, f32[1024,128]{1,0:T(8,128)}, u32[]{:S(2)}) copy-start(f32[1024,128]{1,0:T(8,128)} %get-tuple-element.23) | copy-start | bytes 1572868
  42.3 1.6 %copy-start.3 = (f32[10,1024]{1,0:T(8,128)S(1)}, f32[10,1024]{1,0:T(8,128)}, u32[]{:S(2)}) copy-start(f32[10,1024]{1,0:T(8,128)} %get-tuple-element.14) | copy-start | bytes 122884

commit v3 on v2

--- a/solution.py
+++ b/solution.py
@@ -41,10 +41,10 @@
 def mixer_kernel(
     ring, chips, heads, blocks,
     x_hbm, b_hbm, c_hbm, ld_ref, dy_hbm,
-    y_hbm, dx_hbm, db_hbm, dc_hbm, dg_ref,
+    rounded_out, grads, dg_ref,
     vec, coef, ldp, runc, runr, scale, gain, scaled, pieces, states, states_held, dev, inc, out_state,
-    inner, rounded_out, grads, ptotal, bal, mate_in, far_in, back_in,
-    load_sem, store_sem, grad_store_sem,
+    inner, ptotal, bal, mate_in, far_in, back_in,
+    load_sem,
     chain_send, chain_recv, mate_send, mate_recv, far_send, far_recv, back_send, back_recv,
 ):
     place = lax.axis_index("ctx")
@@ -322,14 +322,6 @@
             else:
                 bal[j] += summed
 
-        @pl.when(d == 0)
-        def _():
-            pltpu.make_async_copy(rounded_out.at[0], y_hbm, store_sem.at[0]).start()
-
-        @pl.when(d == 1)
-        def _():
-            pltpu.make_async_copy(rounded_out.at[1], dx_hbm, store_sem.at[1]).start()
-
     units = blocks * pairs
 
     @pl.loop(units, jnp.maximum(units, HOP_UNITS * hops(first) + CHUNK_UNITS * (pairs - 1) + 1))
@@ -364,39 +356,19 @@
     def _(i):
         far_sum(second, order(second, i))
 
-    def own_store(d, j):
-        target = dc_hbm if d == 0 else db_hbm
-        rows = piece_of(j, own_rows)
-        return pltpu.make_async_copy(grads.at[d, rows, :], target.at[rows, :], grad_store_sem.at[d, j, 0])
-
-    def mate_store(d, j):
-        target = dc_hbm if d == 0 else db_hbm
-        rows = piece_of(j, mate_rows)
-        return pltpu.make_async_copy(back_in.at[d, j], target.at[rows, :], grad_store_sem.at[d, j, 1])
-
     @pl.loop(0, blocks)
     def _(j):
         for d in range(2):
-            own_store(d, j).start()
+            mate_copy(d, j).wait_send()
+            back_copy(d, j).wait_recv()
+            grads[d, piece_of(j, mate_rows), :] = back_in[d, j]
 
     @pl.loop(0, blocks)
     def _(j):
         for d in range(2):
-            back_copy(d, j).wait_recv()
-            mate_store(d, j).start()
-
-    @pl.loop(0, blocks)
-    def _(j):
-        for d in range(2):
-            own_store(d, j).wait()
-            mate_store(d, j).wait()
-            mate_copy(d, j).wait_send()
             back_copy(d, j).wait_send()
             for hop in range(1, chips):
                 far_copy(d, j, hop).wait_send()
-
-    pltpu.make_async_copy(rounded_out.at[0], y_hbm, store_sem.at[0]).wait()
-    pltpu.make_async_copy(rounded_out.at[1], dx_hbm, store_sem.at[1]).wait()
 
     for d in range(2):
 
@@ -405,6 +377,20 @@
             @pl.loop(0, pairs)
             def _(p):
                 chain_copy(d, p).wait_send()
+
+
+def store_kernel(rounded_out, grads, dg_in, y_hbm, dx_hbm, db_hbm, dc_hbm, dg_hbm, sem):
+    copies = [
+        pltpu.make_async_copy(rounded_out.at[0], y_hbm, sem.at[0]),
+        pltpu.make_async_copy(rounded_out.at[1], dx_hbm, sem.at[1]),
+        pltpu.make_async_copy(grads.at[1], db_hbm, sem.at[2]),
+        pltpu.make_async_copy(grads.at[0], dc_hbm, sem.at[3]),
+        pltpu.make_async_copy(dg_in, dg_hbm, sem.at[4]),
+    ]
+    for copy in copies:
+        copy.start()
+    for copy in copies:
+        copy.wait()
 
 
 def per_device(ring, chips, inputs, write_coeffs, read_coeffs, log_decay, out_grad):
@@ -422,19 +408,18 @@
     half = BLOCK // 2
     slots = -(-heads // 16) * 16
     any_spec = pl.BlockSpec(memory_space=pl.ANY)
+    hbm_spec = pl.BlockSpec(memory_space=pltpu.HBM)
     vmem_spec = pl.BlockSpec(memory_space=pltpu.VMEM)
     dma = pltpu.SemaphoreType.DMA
-    y, dx, db, dc, dg = pl.pallas_call(
+    held = pl.pallas_call(
         functools.partial(mixer_kernel, ring, chips, heads, blocks),
         out_shape=(
-            jax.ShapeDtypeStruct((tokens, width), BF16),
-            jax.ShapeDtypeStruct((tokens, width), BF16),
-            jax.ShapeDtypeStruct((tokens, STATE), F32),
-            jax.ShapeDtypeStruct((tokens, STATE), F32),
-            jax.ShapeDtypeStruct((heads, tokens), F32),
+            pltpu.VMEM((2, tokens, width), BF16),
+            pltpu.VMEM((2, tokens, STATE), F32),
+            pltpu.VMEM((heads, tokens), F32),
         ),
-        in_specs=[any_spec, any_spec, any_spec, vmem_spec, any_spec],
-        out_specs=(any_spec, any_spec, any_spec, any_spec, vmem_spec),
+        in_specs=[hbm_spec, hbm_spec, hbm_spec, vmem_spec, hbm_spec],
+        out_specs=(vmem_spec, vmem_spec, vmem_spec),
         scratch_shapes=[
             pltpu.VMEM((2, tokens, width), BF16),
             pltpu.VMEM((2, tokens, STATE), BF16),
@@ -451,16 +436,12 @@
             pltpu.VMEM((2, pairs, STATE, LANES), F32),
             pltpu.VMEM((2, pairs, STATE, LANES), F32),
             pltpu.VMEM((2, tokens, width), F32),
-            pltpu.VMEM((2, tokens, width), BF16),
-            pltpu.VMEM((2, tokens, STATE), F32),
             pltpu.VMEM((2, BLOCK, BLOCK), F32),
             pltpu.VMEM((blocks, slots, BLOCK), F32),
             pltpu.VMEM((2, blocks, half, STATE), F32),
             pltpu.VMEM((2, blocks, chips, half, STATE), F32),
             pltpu.VMEM((2, blocks, half, STATE), F32),
             dma((4,)),
-            dma((2,)),
-            dma((2, blocks, 2)),
             dma((2, pairs)),
             dma((2, pairs)),
             dma((2, blocks)),
@@ -471,9 +452,23 @@
             dma((2, blocks)),
         ],
         compiler_params=pltpu.CompilerParams(
-            collective_id=0, has_side_effects=True, vmem_limit_bytes=56 * 1024 * 1024
+            collective_id=0, has_side_effects=True, vmem_limit_bytes=36 * 1024 * 1024
         ),
     )(inputs, write_coeffs, read_coeffs, log_decay.T, out_grad)
+    y, dx, db, dc, dg = pl.pallas_call(
+        store_kernel,
+        out_shape=(
+            jax.ShapeDtypeStruct((tokens, width), BF16),
+            jax.ShapeDtypeStruct((tokens, width), BF16),
+            jax.ShapeDtypeStruct((tokens, STATE), F32),
+            jax.ShapeDtypeStruct((tokens, STATE), F32),
+            jax.ShapeDtypeStruct((heads, tokens), F32),
+        ),
+        in_specs=[vmem_spec] * 3,
+        out_specs=(any_spec,) * 5,
+        scratch_shapes=[dma((5,))],
+        compiler_params=pltpu.CompilerParams(vmem_limit_bytes=8 * 1024 * 1024),
+    )(*[pltpu.with_memory_space_constraint(piece, pltpu.VMEM) for piece in held])
     dg = dg.T
     if heads > real:
         y = y[:, : real * HEAD_DIM]

time: 44.7 us -> 43.7 us (0.978)
  local copies, waits for them, and re-layouts: 6.18 us -> 5.36 us
    pallas_call x1, Pallas kernels: 37.6 us -> 35.5 us  [per_device(): pl.pallas_call(functools.partial(mixer_kernel, ring, chips, heads, blocks...]
    pallas_call x0 -> x1, Pallas kernels: none -> 1.88 us  [per_device(): pl.pallas_call(store_kernel, out_shape=(jax.ShapeDtypeStruct((tokens, wid...]
    unnamed x13 -> x10, local copies, waits for them, and re-layouts: 6.18 us -> 5.36 us
where the time goes in v3:
time: 43.7 us; the launch traced here: 43.4 us
  Pallas kernels  37.4 us (86%)
  local copies, waits for them, and re-layouts  5.36 us (12%)
  between operations  0.65 us (1%)
    pallas_call x1, Pallas kernels, per_device(): pl.pallas_call(functools.partial(mixer_kernel, ring, chips, heads, blocks...  35.5 us
    unnamed x10, local copies, waits for them, and re-layouts  5.36 us
    pallas_call x1, Pallas kernels, per_device(): pl.pallas_call(store_kernel, out_shape=(jax.ShapeDtypeStruct((tokens, wid...  1.88 us

profile of v3, /device:TPU:0, one launch (start us, length us, event | category | flops | bytes accessed | tf_op | source)
XLA Modules:
  0.0 43.4 jit_solution(15409422818469387653)
XLA Ops:
  0.6 0.0 copy-start
  0.6 1.3 %copy-done = bf16[1024,640]{1,0:T(8,128)(2,1)S(1)} copy-done((bf16[1024,640]{1,0:T(8,128)(2,1)S(1)}, bf16[1024,640]{1,0:T(8,128)(2,1)}, u32[]{:S(2)}) %copy-start) | copy-done | bytes 1310744
  1.9 0.0 copy-start.1
  2.0 1.3 %copy-done.1 = bf16[1024,640]{1,0:T(8,128)(2,1)S(1)} copy-done((bf16[1024,640]{1,0:T(8,128)(2,1)S(1)}, bf16[1024,640]{1,0:T(8,128)(2,1)}, u32[]{:S(2)}) %copy-start.1) | copy-done | bytes 1310744
  3.3 0.0 copy-start.2
  3.3 0.9 %copy-done.2 = bf16[1024,128]{1,0:T(8,128)(2,1)S(1)} copy-done((bf16[1024,128]{1,0:T(8,128)(2,1)S(1)}, bf16[1024,128]{1,0:T(8,128)(2,1)}, u32[]{:S(2)}) %copy-start.2) | copy-done | bytes 262168
  4.2 0.0 copy-start.3
  4.2 0.9 %copy-done.3 = bf16[1024,128]{1,0:T(8,128)(2,1)S(1)} copy-done((bf16[1024,128]{1,0:T(8,128)(2,1)S(1)}, bf16[1024,128]{1,0:T(8,128)(2,1)}, u32[]{:S(2)}) %copy-start.3) | copy-done | bytes 262168
  5.2 0.0 copy-start.4
  5.2 0.8 %copy-done.4 = f32[1024,10]{0,1:T(8,128)S(1)} copy-done((f32[1024,10]{0,1:T(8,128)S(1)}, f32[1024,10]{0,1:T(8,128)}, u32[]{:S(2)}) %copy-start.4) | copy-done | bytes 40984
  6.0 35.5 %shard_map.92 = (bf16[2,1024,640]{2,1,0:T(8,128)(2,1)S(1)}, f32[2,1024,128]{2,1,0:T(8,128)S(1)}, f32[10,1024]{1,0:T(8,128)S(1)}) custom-call(bf16[1024,640]{1,0:T(8,128)(2,1)S(1)} %copy-done, bf16[1024,128]{1,0:T(8,128)(2,1)S(1)} %copy-done.2, bf16[1024,128]{1,0:T(8,128)(2,1)S(1)} %copy-done.3, f32[10,1024]{1,0:T(8,128)S(1)} %bitcast.2, ...), custom_call_target="tpu_custom_call" | custom-call | tf_op jit(solution)/shard_map/pallas_call | solution.py:414
  41.5 1.9 %shard_map.93 = (bf16[1024,640]{1,0:T(8,128)(2,1)}, bf16[1024,640]{1,0:T(8,128)(2,1)}, f32[1024,128]{1,0:T(8,128)}, f32[1024,128]{1,0:T(8,128)}, f32[10,1024]{1,0:T(8,128)}) custom-call(bf16[2,1024,640]{2,1,0:T(8,128)(2,1)S(1)} %get-tuple-element.13.rounded_out, f32[2,1024,128]{2,1,0:T(8,128)S(1)} %get-tuple-element.14.grads, ...), custom_call_target="tpu_custom_call" | custom-call | tf_op jit(solution)/shard_map/pallas_call | solution.py:458
Async XLA Ops:
  0.6 1.3 %copy-start = (bf16[1024,640]{1,0:T(8,128)(2,1)S(1)}, bf16[1024,640]{1,0:T(8,128)(2,1)}, u32[]{:S(2)}) copy-start(bf16[1024,640]{1,0:T(8,128)(2,1)} %x_hbm.1) | copy-start | bytes 3932164
  1.9 1.3 %copy-start.1 = (bf16[1024,640]{1,0:T(8,128)(2,1)S(1)}, bf16[1024,640]{1,0:T(8,128)(2,1)}, u32[]{:S(2)}) copy-start(bf16[1024,640]{1,0:T(8,128)(2,1)} %dy_hbm.1) | copy-start | bytes 3932164
  3.3 0.9 %copy-start.2 = (bf16[1024,128]{1,0:T(8,128)(2,1)S(1)}, bf16[1024,128]{1,0:T(8,128)(2,1)}, u32[]{:S(2)}) copy-start(bf16[1024,128]{1,0:T(8,128)(2,1)} %b_hbm.1) | copy-start | bytes 786436
  4.2 0.9 %copy-start.3 = (bf16[1024,128]{1,0:T(8,128)(2,1)S(1)}, bf16[1024,128]{1,0:T(8,128)(2,1)}, u32[]{:S(2)}) copy-start(bf16[1024,128]{1,0:T(8,128)(2,1)} %c_hbm.1) | copy-start | bytes 786436
  5.2 0.8 %copy-start.4 = (f32[1024,10]{0,1:T(8,128)S(1)}, f32[1024,10]{0,1:T(8,128)}, u32[]{:S(2)}) copy-start(f32[1024,10]{0,1:T(8,128)} %param.8) | copy-start | bytes 122884

commit v4 on v3

--- a/solution.py
+++ b/solution.py
@@ -391,6 +391,10 @@
         copy.start()
     for copy in copies:
         copy.wait()
+
+
+def hbm(array):
+    return pltpu.with_memory_space_constraint(array, pltpu.HBM)
 
 
 def per_device(ring, chips, inputs, write_coeffs, read_coeffs, log_decay, out_grad):
@@ -454,7 +458,7 @@
         compiler_params=pltpu.CompilerParams(
             collective_id=0, has_side_effects=True, vmem_limit_bytes=36 * 1024 * 1024
         ),
-    )(inputs, write_coeffs, read_coeffs, log_decay.T, out_grad)
+    )(hbm(inputs), hbm(write_coeffs), hbm(read_coeffs), log_decay.T, hbm(out_grad))
     y, dx, db, dc, dg = pl.pallas_call(
         store_kernel,
         out_shape=(

time: 43.7 us -> 38.9 us (0.89)
  local copies, waits for them, and re-layouts: 5.36 us -> 0.83 us
    unnamed x10 -> x2, local copies, waits for them, and re-layouts: 5.36 us -> 0.83 us
where the time goes in v4:
time: 38.9 us; the launch traced here: 38.7 us
  Pallas kernels  37.2 us (96%)
  local copies, waits for them, and re-layouts  0.83 us (2%)
  between operations  0.65 us (2%)
    pallas_call x1, Pallas kernels, per_device(): pl.pallas_call(functools.partial(mixer_kernel, ring, chips, heads, blocks...  35.3 us
    pallas_call x1, Pallas kernels, per_device(): pl.pallas_call(store_kernel, out_shape=(jax.ShapeDtypeStruct((tokens, wid...  1.88 us
    unnamed x2, local copies, waits for them, and re-layouts  0.83 us

profile of v4, /device:TPU:0, one launch (start us, length us, event | category | flops | bytes accessed | tf_op | source)
XLA Modules:
  0.0 38.7 jit_solution(5715779181848143218)
XLA Ops:
  0.6 0.0 copy-start
  0.6 0.8 %copy-done = f32[1024,10]{0,1:T(8,128)S(1)} copy-done((f32[1024,10]{0,1:T(8,128)S(1)}, f32[1024,10]{0,1:T(8,128)}, u32[]{:S(2)}) %copy-start) | copy-done | bytes 40984
  1.5 35.3 %shard_map.92 = (bf16[2,1024,640]{2,1,0:T(8,128)(2,1)S(1)}, f32[2,1024,128]{2,1,0:T(8,128)S(1)}, f32[10,1024]{1,0:T(8,128)S(1)}) custom-call(bf16[1024,640]{1,0:T(8,128)(2,1)} %x_hbm.1, bf16[1024,128]{1,0:T(8,128)(2,1)} %b_hbm.1, bf16[1024,128]{1,0:T(8,128)(2,1)} %c_hbm.1, f32[10,1024]{1,0:T(8,128)S(1)} %bitcast.2, bf16[1024,640]{1,0:T(8,128)(2,1)} %dy_hbm.1), custom_call_target="tpu_custom_call" | custom-call | tf_op jit(solution)/shard_map/pallas_call | solution.py:418
  36.8 1.9 %shard_map.93 = (bf16[1024,640]{1,0:T(8,128)(2,1)}, bf16[1024,640]{1,0:T(8,128)(2,1)}, f32[1024,128]{1,0:T(8,128)}, f32[1024,128]{1,0:T(8,128)}, f32[10,1024]{1,0:T(8,128)}) custom-call(bf16[2,1024,640]{2,1,0:T(8,128)(2,1)S(1)} %get-tuple-element.13.rounded_out, f32[2,1024,128]{2,1,0:T(8,128)S(1)} %get-tuple-element.14.grads, ...), custom_call_target="tpu_custom_call" | custom-call | tf_op jit(solution)/shard_map/pallas_call | solution.py:462
Async XLA Ops:
  0.6 0.8 %copy-start = (f32[1024,10]{0,1:T(8,128)S(1)}, f32[1024,10]{0,1:T(8,128)}, u32[]{:S(2)}) copy-start(f32[1024,10]{0,1:T(8,128)} %param.8) | copy-start | bytes 122884
